TPU v7x, 256 devices: a whole 4x4x8 slice. The times are simulated.
256 devices in a mesh: prow: 32 (over y, z), pcol: 8 (over x, core).
Axes of the slice: x: 4, y: 4, z: 8, core: 2. Of those that a mesh axis runs over, the one named last changes fastest.
Arguments:
- right_side: bfloat16 [32, 6, 128, 256], P('prow'), may hold values from -6 to 6
- lower_inverse: bfloat16 [32, 6, 256, 256], P('prow'), as said below
- upper_inverse: bfloat16 [32, 6, 256, 256], P('prow'), as said below
- lower_blocks: bfloat16 [32, 5, 48, 256, 256], P('prow', None, 'pcol'), may hold values from -0.0546875 to 0.0546875
- lower_sources: int32 [32, 5, 48], P('prow', None, 'pcol'), may hold values from 0 to 159, as said below
- lower_counts: int32 [32, 5, 8], P('prow', None, 'pcol'), may hold values from 1 to 6, as said below
- upper_blocks: bfloat16 [32, 5, 48, 256, 256], P('prow', None, 'pcol'), may hold values from -0.0546875 to 0.0546875
- upper_sources: int32 [32, 5, 48], P('prow', None, 'pcol'), may hold values from 32 to 191, as said below
- upper_counts: int32 [32, 5, 8], P('prow', None, 'pcol'), may hold values from 1 to 6, as said below
Outputs:
- solution: bfloat16 [32, 6, 128, 256], P('prow')
Inputs may be any that keep to these rules, and one draw needn't show every extreme that they name: `lower_sources`: entry [r, l, c] names supernode v * 32 + p of a level v below l + 1, with p % (8) == c // 6; entries may repeat. `upper_sources`: entry [r, l, c] names supernode v * 32 + p of a level v above l, with p % (8) == c // 6; entries may repeat. `lower_counts`: entry [r, l, g] is how many of the 6 slots of group g are live; the live ones come first. `upper_counts`: entry [r, l, g] is how many of the 6 slots of group g are live; the live ones come first. `lower_inverse`: each block is lower triangular. `upper_inverse`: each block is upper triangular.
All inputs are finite; a program needn't handle non-finite values.
Results may differ from a plain program's by a relative error of at most 0.02.
Values may be sent and summed in bfloat16 or wider, within the bound.
No kernel may reach another device: no remote copies, remote signals or barrier semaphores. Data moves between devices by JAX's collectives and lax.ppermute only.
A program may use at most 64 MiB of HBM per device.

v0:
```python
import jax
import jax.numpy as jnp
from jax import lax
from jax.sharding import PartitionSpec as P


def pick_sources(sources, count, store, width, ncol):
    group = store.shape[1]
    flat = store.reshape(store.shape[0] * group, store.shape[2], store.shape[3])
    position = sources // width * group + sources % width // ncol
    picked = flat[position]
    live = jnp.arange(sources.shape[0], dtype=jnp.int32) < count
    return jnp.where(live[:, None, None], picked, jnp.zeros_like(picked))


def contract(picked, blocks):
    return lax.dot_general(
        picked, blocks, (((0, 2), (0, 2)), ((), ())), preferred_element_type=jnp.float32
    )


def apply_inverse(residual, inverse):
    product = lax.dot_general(
        residual, inverse, (((1,), (1,)), ((), ())), preferred_element_type=jnp.float32
    )
    return product.astype(jnp.bfloat16)


def solve_level(right, inverse, blocks, sources, count, store):
    width = lax.axis_size("prow")
    ncol = lax.axis_size("pcol")
    picked = pick_sources(sources, count, store, width, ncol)
    total = lax.psum(contract(picked, blocks), "pcol")
    residual = (right.astype(jnp.float32) - total).astype(jnp.bfloat16)
    return apply_inverse(residual, inverse)


def spread(solved):
    ncol = lax.axis_size("pcol")
    column = lax.axis_index("pcol")
    whole = lax.all_gather(solved[None], "prow", axis=0, tiled=True)
    whole = whole.reshape(whole.shape[0] // ncol, ncol, whole.shape[1], whole.shape[2])
    return lax.dynamic_index_in_dim(whole, column, 1, keepdims=False)


def shards(
    right_side,
    lower_inverse,
    upper_inverse,
    lower_blocks,
    lower_sources,
    lower_counts,
    upper_blocks,
    upper_sources,
    upper_counts,
):
    group = lax.axis_size("prow") // lax.axis_size("pcol")
    levels = right_side.shape[1]
    shape = (levels, group, right_side.shape[2], right_side.shape[3])
    forward_store = jnp.zeros(shape, jnp.bfloat16)
    forward_own = []
    for level in range(levels):
        if level == 0:
            solved = apply_inverse(right_side[0, 0], lower_inverse[0, 0])
        else:
            solved = solve_level(
                right_side[0, level],
                lower_inverse[0, level],
                lower_blocks[0, level - 1],
                lower_sources[0, level - 1],
                lower_counts[0, level - 1, 0],
                forward_store,
            )
        forward_own.append(solved)
        if level + 1 < levels:
            forward_store = forward_store.at[level].set(spread(solved))
    backward_store = jnp.zeros(shape, jnp.bfloat16)
    backward_own = [None] * levels
    for level in range(levels - 1, -1, -1):
        if level == levels - 1:
            solved = apply_inverse(forward_own[level], upper_inverse[0, level])
        else:
            solved = solve_level(
                forward_own[level],
                upper_inverse[0, level],
                upper_blocks[0, level],
                upper_sources[0, level],
                upper_counts[0, level, 0],
                backward_store,
            )
        backward_own[level] = solved
        if level > 0:
            backward_store = backward_store.at[level].set(spread(solved))
    return jnp.stack(backward_own)[None]


def solution(mesh):
    in_specs = (
        P("prow", None, None, None),
        P("prow", None, None, None),
        P("prow", None, None, None),
        P("prow", None, "pcol", None, None),
        P("prow", None, "pcol"),
        P("prow", None, "pcol"),
        P("prow", None, "pcol", None, None),
        P("prow", None, "pcol"),
        P("prow", None, "pcol"),
    )
    out_specs = P("prow", None, None, None)
    return jax.shard_map(shards, mesh=mesh, in_specs=in_specs, out_specs=out_specs, check_vma=False)
```

profile of v0, /device:TPU:8, one launch (start us, length us, event | category | flops | bytes accessed | tf_op | source)
XLA Modules:
  0.0 1472.5 jit_solution(6980355928719453003)
XLA Ops:
  6.5 1.8 convolution_convert_fusion.11
  8.4 1.5 fusion.124
  9.9 0.6 iota_compare_fusion.7
  10.6 1.4 fusion.107
  12.0 77.6 %all-gather.21.cloned.1.call-done = bf16[4096,256]{1,0:T(8,128)(2,1)} async-done(((bf16[128,256]{1,0:T(8,128)(2,1)}), bf16[4096,256]{1,0:T(8,128)(2,1)}) %all-gather.21.cloned.1.call-update) | async-done | bytes 2097168 | tf_op jit(solution)/shard_map/all_gather | solution.py:41
  89.6 1.0 dynamic-slice_bitcast_fusion.1
  91.3 2.2 convolution_bitcast_fusion.9
  93.6 62.8 %all-reduce.13.cloned.1.call-done = f32[128,256]{1,0:T(8,128)} async-done(((f32[128,256]{1,0:T(8,128)}), f32[128,256]{1,0:T(8,128)}) %all-reduce.13.cloned.1.call-update) | async-done | bytes 131088 | tf_op jit(solution)/shard_map/psum | solution.py:33
  156.4 1.7 convolution_convert_fusion.10
  158.2 0.7 iota_compare_fusion.6
  159.0 76.3 %all-gather.23.cloned.1.call-done = bf16[4096,256]{1,0:T(8,128)(2,1)} async-done(((bf16[128,256]{1,0:T(8,128)(2,1)}), bf16[4096,256]{1,0:T(8,128)(2,1)}) %all-gather.23.cloned.1.call-update) | async-done | bytes 2097168 | tf_op jit(solution)/shard_map/all_gather | solution.py:41
  235.2 1.0 bitcast_dynamic-update-slice_fusion.7
  236.8 2.2 convolution_bitcast_fusion.8
  239.1 62.8 %all-reduce.15.cloned.1.call-done = f32[128,256]{1,0:T(8,128)} async-done(((f32[128,256]{1,0:T(8,128)}), f32[128,256]{1,0:T(8,128)}) %all-reduce.15.cloned.1.call-update) | async-done | bytes 131088 | tf_op jit(solution)/shard_map/psum | solution.py:33
  301.9 1.7 convolution_convert_fusion.9
  303.7 0.7 iota_compare_fusion.5
  304.4 75.8 %all-gather.25.cloned.1.call-done = bf16[4096,256]{1,0:T(8,128)(2,1)} async-done(((bf16[128,256]{1,0:T(8,128)(2,1)}), bf16[4096,256]{1,0:T(8,128)(2,1)}) %all-gather.25.cloned.1.call-update) | async-done | bytes 2097168 | tf_op jit(solution)/shard_map/all_gather | solution.py:41
  380.2 1.0 bitcast_dynamic-update-slice_fusion.6
  381.7 2.2 convolution_bitcast_fusion.7
  384.0 62.8 %all-reduce.17.cloned.1.call-done = f32[128,256]{1,0:T(8,128)} async-done(((f32[128,256]{1,0:T(8,128)}), f32[128,256]{1,0:T(8,128)}) %all-reduce.17.cloned.1.call-update) | async-done | bytes 131088 | tf_op jit(solution)/shard_map/psum | solution.py:33
  446.8 1.7 convolution_convert_fusion.8
  449.3 76.3 %all-gather.27.cloned.1.call-done = bf16[4096,256]{1,0:T(8,128)(2,1)} async-done(((bf16[128,256]{1,0:T(8,128)(2,1)}), bf16[4096,256]{1,0:T(8,128)(2,1)}) %all-gather.27.cloned.1.call-update) | async-done | bytes 2097168 | tf_op jit(solution)/shard_map/all_gather | solution.py:41
  525.6 1.0 bitcast_dynamic-update-slice_fusion.5
  527.2 2.2 convolution_bitcast_fusion.6
  529.4 62.8 %all-reduce.19.cloned.1.call-done = f32[128,256]{1,0:T(8,128)} async-done(((f32[128,256]{1,0:T(8,128)}), f32[128,256]{1,0:T(8,128)}) %all-reduce.19.cloned.1.call-update) | async-done | bytes 131088 | tf_op jit(solution)/shard_map/psum | solution.py:33
  592.2 1.7 convolution_convert_fusion.7
  594.0 1.1 iota_compare_fusion.8
  595.1 0.7 pad_clamp_fusion.5
  595.8 74.9 %all-gather.29.cloned.1.call-done = bf16[4096,256]{1,0:T(8,128)(2,1)} async-done(((bf16[128,256]{1,0:T(8,128)(2,1)}), bf16[4096,256]{1,0:T(8,128)(2,1)}) %all-gather.29.cloned.1.call-update) | async-done | bytes 2097168 | tf_op jit(solution)/shard_map/all_gather | solution.py:41
  670.7 1.0 bitcast_dynamic-update-slice_fusion.4
  672.3 2.2 convolution_bitcast_fusion.5
  674.5 62.8 %all-reduce.21.cloned.1.call-done = f32[128,256]{1,0:T(8,128)} async-done(((f32[128,256]{1,0:T(8,128)}), f32[128,256]{1,0:T(8,128)}) %all-reduce.21.cloned.1.call-update) | async-done | bytes 131088 | tf_op jit(solution)/shard_map/psum | solution.py:33
  737.4 1.9 convolution_convert_fusion.5
  739.3 0.7 fusion.123
  740.0 0.6 iota_compare_fusion.3
  740.6 0.6 pad_clamp_fusion.4
  741.3 74.9 %all-gather.31.cloned.1.call-done = bf16[4096,256]{1,0:T(8,128)(2,1)} async-done(((bf16[128,256]{1,0:T(8,128)(2,1)}), bf16[4096,256]{1,0:T(8,128)(2,1)}) %all-gather.31.cloned.1.call-update) | async-done | bytes 2097168 | tf_op jit(solution)/shard_map/all_gather | solution.py:41
  816.2 1.0 dynamic-slice_bitcast_fusion
  817.9 2.2 convolution_bitcast_fusion.4
  820.2 62.8 %all-reduce.23.cloned.1.call-done = f32[128,256]{1,0:T(8,128)} async-done(((f32[128,256]{1,0:T(8,128)}), f32[128,256]{1,0:T(8,128)}) %all-reduce.23.cloned.1.call-update) | async-done | bytes 131088 | tf_op jit(solution)/shard_map/psum | solution.py:33
  883.0 1.7 convolution_convert_fusion.4
  884.8 0.7 iota_compare_fusion.2
  885.5 75.9 %all-gather.33.cloned.1.call-done = bf16[4096,256]{1,0:T(8,128)(2,1)} async-done(((bf16[128,256]{1,0:T(8,128)(2,1)}), bf16[4096,256]{1,0:T(8,128)(2,1)}) %all-gather.33.cloned.1.call-update) | async-done | bytes 2097168 | tf_op jit(solution)/shard_map/all_gather | solution.py:41
  961.4 1.0 bitcast_dynamic-update-slice_fusion.3
  963.0 2.2 convolution_bitcast_fusion.3
  965.3 62.8 %all-reduce.25.cloned.1.call-done = f32[128,256]{1,0:T(8,128)} async-done(((f32[128,256]{1,0:T(8,128)}), f32[128,256]{1,0:T(8,128)}) %all-reduce.25.cloned.1.call-update) | async-done | bytes 131088 | tf_op jit(solution)/shard_map/psum | solution.py:33
  1028.1 1.7 convolution_convert_fusion.3
  1030.5 76.2 %all-gather.35.cloned.1.call-done = bf16[4096,256]{1,0:T(8,128)(2,1)} async-done(((bf16[128,256]{1,0:T(8,128)(2,1)}), bf16[4096,256]{1,0:T(8,128)(2,1)}) %all-gather.35.cloned.1.call-update) | async-done | bytes 2097168 | tf_op jit(solution)/shard_map/all_gather | solution.py:41
  1106.7 1.0 bitcast_dynamic-update-slice_fusion.2
  1108.3 2.2 convolution_bitcast_fusion.2
  1110.6 62.8 %all-reduce.27.cloned.1.call-done = f32[128,256]{1,0:T(8,128)} async-done(((f32[128,256]{1,0:T(8,128)}), f32[128,256]{1,0:T(8,128)}) %all-reduce.27.cloned.1.call-update) | async-done | bytes 131088 | tf_op jit(solution)/shard_map/psum | solution.py:33
  1173.4 1.7 convolution_convert_fusion.2
  1175.8 75.9 %all-gather.37.cloned.1.call-done = bf16[4096,256]{1,0:T(8,128)(2,1)} async-done(((bf16[128,256]{1,0:T(8,128)(2,1)}), bf16[4096,256]{1,0:T(8,128)(2,1)}) %all-gather.37.cloned.1.call-update) | async-done | bytes 2097168 | tf_op jit(solution)/shard_map/all_gather | solution.py:41
  1251.7 1.0 bitcast_dynamic-update-slice_fusion.1
  1253.2 2.2 convolution_bitcast_fusion.1
  1255.5 62.8 %all-reduce.29.cloned.1.call-done = f32[128,256]{1,0:T(8,128)} async-done(((f32[128,256]{1,0:T(8,128)}), f32[128,256]{1,0:T(8,128)}) %all-reduce.29.cloned.1.call-update) | async-done | bytes 131088 | tf_op jit(solution)/shard_map/psum | solution.py:33
  1318.3 1.7 convolution_convert_fusion.1
  1320.1 0.7 iota_compare_fusion.9
  1320.8 76.3 %all-gather.39.cloned.1.call-done = bf16[4096,256]{1,0:T(8,128)(2,1)} async-done(((bf16[128,256]{1,0:T(8,128)(2,1)}), bf16[4096,256]{1,0:T(8,128)(2,1)}) %all-gather.39.cloned.1.call-update) | async-done | bytes 2097168 | tf_op jit(solution)/shard_map/all_gather | solution.py:41
  1397.1 1.0 bitcast_dynamic-update-slice_fusion
  1398.7 2.2 convolution_bitcast_fusion
  1400.9 62.8 %all-reduce.31.cloned.1.call-done = f32[128,256]{1,0:T(8,128)} async-done(((f32[128,256]{1,0:T(8,128)}), f32[128,256]{1,0:T(8,128)}) %all-reduce.31.cloned.1.call-update) | async-done | bytes 131088 | tf_op jit(solution)/shard_map/psum | solution.py:33
  1463.7 1.1 fusion.1
  1465.0 0.7 copy-done.14
  (101 shorter events, 9.1 us)
Async XLA Ops:
  6.5 83.1 %all-gather.21.cloned.1.call-start = ((), (), s32[]{:S(2)}) async-start(), calls=%async_computation.10 | async-start | bytes 2162688 | tf_op jit(solution)/shard_map/all_gather | solution.py:41
  8.3 148.1 %all-reduce.13.cloned.1.call-start = ((), (), s32[]{:S(2)}) async-start(), calls=%async_computation | async-start | bytes 262144 | tf_op jit(solution)/shard_map/psum | solution.py:33
  90.6 65.9 %copy-start.1 = (bf16[1,6,256,256]{3,2,1,0:T(8,128)(2,1)S(1)}, bf16[1,6,256,256]{3,2,1,0:T(8,128)(2,1)}, u32[]{:S(2)}) copy-start(bf16[1,6,256,256]{3,2,1,0:T(8,128)(2,1)} %param.30) | copy-start | bytes 2359300
  90.6 65.8 %copy-start.12 = (bf16[1,6,128,256]{3,2,1,0:T(8,128)(2,1)S(1)}, bf16[1,6,128,256]{3,2,1,0:T(8,128)(2,1)}, u32[]{:S(2)}) copy-start(bf16[1,6,128,256]{3,2,1,0:T(8,128)(2,1)} %param.29) | copy-start | bytes 1179652
  93.6 141.7 %all-gather.23.cloned.1.call-start = ((), (), s32[]{:S(2)}) async-start(), calls=%async_computation.11 | async-start | bytes 2162688 | tf_op jit(solution)/shard_map/all_gather | solution.py:41
  158.2 143.7 %all-reduce.15.cloned.1.call-start = ((), (), s32[]{:S(2)}) async-start(), calls=%async_computation.1 | async-start | bytes 262144 | tf_op jit(solution)/shard_map/psum | solution.py:33
  239.0 141.2 %all-gather.25.cloned.1.call-start = ((), (), s32[]{:S(2)}) async-start(), calls=%async_computation.12 | async-start | bytes 2162688 | tf_op jit(solution)/shard_map/all_gather | solution.py:41
  303.6 143.2 %all-reduce.17.cloned.1.call-start = ((), (), s32[]{:S(2)}) async-start(), calls=%async_computation.2 | async-start | bytes 262144 | tf_op jit(solution)/shard_map/psum | solution.py:33
  383.9 141.7 %all-gather.27.cloned.1.call-start = ((), (), s32[]{:S(2)}) async-start(), calls=%async_computation.13 | async-start | bytes 2162688 | tf_op jit(solution)/shard_map/all_gather | solution.py:41
  448.6 143.7 %all-reduce.19.cloned.1.call-start = ((), (), s32[]{:S(2)}) async-start(), calls=%async_computation.3 | async-start | bytes 262144 | tf_op jit(solution)/shard_map/psum | solution.py:33
  529.3 208.0 %copy-start = (bf16[1,6,256,256]{3,2,1,0:T(8,128)(2,1)S(1)}, bf16[1,6,256,256]{3,2,1,0:T(8,128)(2,1)}, u32[]{:S(2)}) copy-start(bf16[1,6,256,256]{3,2,1,0:T(8,128)(2,1)} %param.31) | copy-start | bytes 2359300
  529.4 209.9 %copy-start.13 = (s32[1,5,1]{1,2,0:T(1,128)S(1)}, s32[1,5,1]{1,2,0:T(1,128)}, u32[]{:S(2)}) copy-start(s32[1,5,1]{1,2,0:T(1,128)} %param.37) | copy-start | bytes 64
  529.4 141.3 %all-gather.29.cloned.1.call-start = ((), (), s32[]{:S(2)}) async-start(), calls=%async_computation.14 | async-start | bytes 2162688 | tf_op jit(solution)/shard_map/all_gather | solution.py:41
  594.0 143.4 %all-reduce.21.cloned.1.call-start = ((), (), s32[]{:S(2)}) async-start(), calls=%async_computation.4 | async-start | bytes 262144 | tf_op jit(solution)/shard_map/psum | solution.py:33
  674.5 141.7 %all-gather.31.cloned.1.call-start = ((), (), s32[]{:S(2)}) async-start(), calls=%async_computation.15 | async-start | bytes 2162688 | tf_op jit(solution)/shard_map/all_gather | solution.py:41
  739.2 143.7 %all-reduce.23.cloned.1.call-start = ((), (), s32[]{:S(2)}) async-start(), calls=%async_computation.5 | async-start | bytes 262144 | tf_op jit(solution)/shard_map/psum | solution.py:33
  817.1 65.9 %copy-start.10 = (bf16[128,256]{1,0:T(8,128)(2,1)S(1)}, bf16[128,256]{1,0:T(8,128)(2,1)}, u32[]{:S(2)}) copy-start(bf16[128,256]{1,0:T(8,128)(2,1)} %convolution_convert_fusion.7) | copy-start | bytes 196612
  817.1 68.3 %copy-start.16 = (s32[6]{0:T(128)S(1)}, s32[6]{0:T(128)}, u32[]{:S(2)}) copy-start(s32[6]{0:T(128)} %get-tuple-element.147) | copy-start | bytes 76
  820.1 208.0 %copy-start.9 = (bf16[128,256]{1,0:T(8,128)(2,1)S(1)}, bf16[128,256]{1,0:T(8,128)(2,1)}, u32[]{:S(2)}) copy-start(bf16[128,256]{1,0:T(8,128)(2,1)} %convolution_convert_fusion.8) | copy-start | bytes 196612
  820.1 210.4 %copy-start.15 = (s32[6]{0:T(128)S(1)}, s32[6]{0:T(128)}, u32[]{:S(2)}) copy-start(s32[6]{0:T(128)} %get-tuple-element.148) | copy-start | bytes 76
  820.1 141.3 %all-gather.33.cloned.1.call-start = ((), (), s32[]{:S(2)}) async-start(), calls=%async_computation.16 | async-start | bytes 2162688 | tf_op jit(solution)/shard_map/all_gather | solution.py:41
  884.7 143.3 %all-reduce.25.cloned.1.call-start = ((), (), s32[]{:S(2)}) async-start(), calls=%async_computation.6 | async-start | bytes 262144 | tf_op jit(solution)/shard_map/psum | solution.py:33
  965.2 208.2 %copy-start.8 = (bf16[128,256]{1,0:T(8,128)(2,1)S(1)}, bf16[128,256]{1,0:T(8,128)(2,1)}, u32[]{:S(2)}) copy-start(bf16[128,256]{1,0:T(8,128)(2,1)} %convolution_convert_fusion.9) | copy-start | bytes 196612
  965.2 141.5 %all-gather.35.cloned.1.call-start = ((), (), s32[]{:S(2)}) async-start(), calls=%async_computation.17 | async-start | bytes 2162688 | tf_op jit(solution)/shard_map/all_gather | solution.py:41
  1029.8 143.5 %all-reduce.27.cloned.1.call-start = ((), (), s32[]{:S(2)}) async-start(), calls=%async_computation.7 | async-start | bytes 262144 | tf_op jit(solution)/shard_map/psum | solution.py:33
  1110.5 207.8 %copy-start.7 = (bf16[128,256]{1,0:T(8,128)(2,1)S(1)}, bf16[128,256]{1,0:T(8,128)(2,1)}, u32[]{:S(2)}) copy-start(bf16[128,256]{1,0:T(8,128)(2,1)} %convolution_convert_fusion.10) | copy-start | bytes 196612
  1110.5 141.2 %all-gather.37.cloned.1.call-start = ((), (), s32[]{:S(2)}) async-start(), calls=%async_computation.18 | async-start | bytes 2162688 | tf_op jit(solution)/shard_map/all_gather | solution.py:41
  1175.1 143.2 %all-reduce.29.cloned.1.call-start = ((), (), s32[]{:S(2)}) async-start(), calls=%async_computation.8 | async-start | bytes 262144 | tf_op jit(solution)/shard_map/psum | solution.py:33
  1255.4 208.3 %copy-start.6 = (bf16[128,256]{1,0:T(8,128)(2,1)S(1)}, bf16[128,256]{1,0:T(8,128)(2,1)}, u32[]{:S(2)}) copy-start(bf16[128,256]{1,0:T(8,128)(2,1)} %convolution_convert_fusion.11) | copy-start | bytes 196612
  1255.5 209.4 %copy-start.4 = (bf16[128,256]{1,0:T(8,128)(2,1)S(1)}, bf16[128,256]{1,0:T(8,128)(2,1)}, u32[]{:S(2)}) copy-start(bf16[128,256]{1,0:T(8,128)(2,1)} %convolution_convert_fusion.2) | copy-start | bytes 196612
  1255.5 209.4 %copy-start.3 = (bf16[128,256]{1,0:T(8,128)(2,1)S(1)}, bf16[128,256]{1,0:T(8,128)(2,1)}, u32[]{:S(2)}) copy-start(bf16[128,256]{1,0:T(8,128)(2,1)} %convolution_convert_fusion.3) | copy-start | bytes 196612
  1255.5 141.6 %all-gather.39.cloned.1.call-start = ((), (), s32[]{:S(2)}) async-start(), calls=%async_computation.19 | async-start | bytes 2162688 | tf_op jit(solution)/shard_map/all_gather | solution.py:41
  1320.1 144.8 %copy-start.5 = (bf16[128,256]{1,0:T(8,128)(2,1)S(1)}, bf16[128,256]{1,0:T(8,128)(2,1)}, u32[]{:S(2)}) copy-start(bf16[128,256]{1,0:T(8,128)(2,1)} %convolution_convert_fusion.1) | copy-start | bytes 196612
  1320.1 144.9 %copy-start.2 = (bf16[128,256]{1,0:T(8,128)(2,1)S(1)}, bf16[128,256]{1,0:T(8,128)(2,1)}, u32[]{:S(2)}) copy-start(bf16[128,256]{1,0:T(8,128)(2,1)} %convolution_convert_fusion.4) | copy-start | bytes 196612
  1320.1 144.9 %copy-start.11 = (bf16[128,256]{1,0:T(8,128)(2,1)S(1)}, bf16[128,256]{1,0:T(8,128)(2,1)}, u32[]{:S(2)}) copy-start(bf16[128,256]{1,0:T(8,128)(2,1)} %convolution_convert_fusion.5) | copy-start | bytes 196612
  1320.1 143.6 %all-reduce.31.cloned.1.call-start = ((), (), s32[]{:S(2)}) async-start(), calls=%async_computation.9 | async-start | bytes 262144 | tf_op jit(solution)/shard_map/psum | solution.py:33
  1465.0 0.7 copy-start.14
Sparse Core Ops, SparseCore 0:
  9.9 79.6 all-gather.20
  93.7 62.6 all-reduce.12
  159.4 75.8 all-gather.22
  239.1 62.6 all-reduce.14
  304.3 75.8 all-gather.24
  384.1 62.6 all-reduce.16
  449.7 75.8 all-gather.26
  529.5 62.6 all-reduce.18
  594.8 75.8 all-gather.28
  674.6 62.6 all-reduce.20
  740.3 75.8 all-gather.30
  820.2 62.7 all-reduce.22
  885.6 75.8 all-gather.32
  965.3 62.6 all-reduce.24
  1030.9 75.8 all-gather.34
  1110.6 62.6 all-reduce.26
  1175.8 75.8 all-gather.36
  1255.6 62.6 all-reduce.28
  1321.2 75.8 all-gather.38
  1401.0 62.6 all-reduce.30
where the time goes:
time: 1470 us
  waiting for transfers between devices  1390 us (95%)
  matrix products  40.5 us (3%)
  local copies, waits for them, and re-layouts  18.7 us (1%)
    all_gather x10, waiting for transfers between devices, spread(): whole = lax.all_gather(solved[None], 'prow', axis=0, tiled=True)  760 us
    psum x10, waiting for transfers between devices, solve_level(): total = lax.psum(contract(picked, blocks), 'pcol')  628 us
  transfers between devices with their start and end apart: 20, of which 20 were waited for; matrix products, arithmetic and copies ran while one was open for 1% of the time, Pallas kernels for 0%

commit v1 on v0

--- a/solution.py
+++ b/solution.py
@@ -30,7 +30,7 @@
     width = lax.axis_size("prow")
     ncol = lax.axis_size("pcol")
     picked = pick_sources(sources, count, store, width, ncol)
-    total = lax.psum(contract(picked, blocks), "pcol")
+    total = jnp.sum(lax.all_gather(contract(picked, blocks), "pcol"), axis=0)
     residual = (right.astype(jnp.float32) - total).astype(jnp.bfloat16)
     return apply_inverse(residual, inverse)
 

time: 1470 us -> 1100 us (0.75)
  waiting for transfers between devices: 1390 us -> 1010 us
    psum x10 -> x0, waiting for transfers between devices: 628 us -> none  [solve_level(): total = lax.psum(contract(picked, blocks), 'pcol')]
    all_gather x0 -> x10, waiting for transfers between devices: none -> 244 us  [solve_level(): total = jnp.sum(lax.all_gather(contract(picked, blocks), 'pcol'), axis=0)]
where the time goes in v1:
time: 1100 us
  waiting for transfers between devices  1010 us (92%)
  matrix products  32.3 us (3%)
  other arithmetic  21.3 us (2%)
  local copies, waits for them, and re-layouts  19 us (2%)
  between operations  14.3 us (1%)
    all_gather x10, waiting for transfers between devices, spread(): whole = lax.all_gather(solved[None], 'prow', axis=0, tiled=True)  763 us
    all_gather x10, waiting for transfers between devices, solve_level(): total = jnp.sum(lax.all_gather(contract(picked, blocks), 'pcol'), axis=0)  244 us
  transfers between devices with their start and end apart: 20, of which 20 were waited for; matrix products, arithmetic and copies ran while one was open for 1% of the time, Pallas kernels for 0%

profile of v1, /device:TPU:8, one launch (start us, length us, event | category | flops | bytes accessed | tf_op | source)
XLA Modules:
  0.0 1095.3 jit_solution(10023883318430683575)
XLA Ops:
  6.5 1.8 convolution_convert_fusion.11
  8.4 1.5 fusion.123
  10.6 1.4 fusion.106
  12.0 77.6 %all-gather.41.cloned.1.call-done = bf16[4096,256]{1,0:T(8,128)(2,1)} async-done(((bf16[128,256]{1,0:T(8,128)(2,1)}), bf16[4096,256]{1,0:T(8,128)(2,1)}) %all-gather.41.cloned.1.call-update) | async-done | bytes 2097168 | tf_op jit(solution)/shard_map/all_gather | solution.py:41
  89.6 1.0 dynamic-slice_bitcast_fusion.1
  91.3 2.2 convolution_bitcast_fusion.9
  93.6 24.4 %all-gather.43.cloned.1.call-done = f32[1024,256]{1,0:T(8,128)} async-done(((f32[128,256]{1,0:T(8,128)}), f32[1024,256]{1,0:T(8,128)}) %all-gather.43.cloned.1.call-update) | async-done | bytes 1048592 | tf_op jit(solution)/shard_map/all_gather | solution.py:33
  118.0 1.3 reduce_sum.100
  119.3 0.8 convolution_convert_fusion.10
  120.8 76.5 %all-gather.45.cloned.1.call-done = bf16[4096,256]{1,0:T(8,128)(2,1)} async-done(((bf16[128,256]{1,0:T(8,128)(2,1)}), bf16[4096,256]{1,0:T(8,128)(2,1)}) %all-gather.45.cloned.1.call-update) | async-done | bytes 2097168 | tf_op jit(solution)/shard_map/all_gather | solution.py:41
  197.3 1.0 bitcast_dynamic-update-slice_fusion.7
  198.8 2.2 convolution_bitcast_fusion.8
  201.1 24.4 %all-gather.47.cloned.1.call-done = f32[1024,256]{1,0:T(8,128)} async-done(((f32[128,256]{1,0:T(8,128)}), f32[1024,256]{1,0:T(8,128)}) %all-gather.47.cloned.1.call-update) | async-done | bytes 1048592 | tf_op jit(solution)/shard_map/all_gather | solution.py:33
  225.5 1.3 reduce_sum.102
  226.8 0.8 convolution_convert_fusion.9
  228.4 76.2 %all-gather.49.cloned.1.call-done = bf16[4096,256]{1,0:T(8,128)(2,1)} async-done(((bf16[128,256]{1,0:T(8,128)(2,1)}), bf16[4096,256]{1,0:T(8,128)(2,1)}) %all-gather.49.cloned.1.call-update) | async-done | bytes 2097168 | tf_op jit(solution)/shard_map/all_gather | solution.py:41
  304.6 1.0 bitcast_dynamic-update-slice_fusion.6
  306.2 2.2 convolution_bitcast_fusion.7
  308.4 24.4 %all-gather.51.cloned.1.call-done = f32[1024,256]{1,0:T(8,128)} async-done(((f32[128,256]{1,0:T(8,128)}), f32[1024,256]{1,0:T(8,128)}) %all-gather.51.cloned.1.call-update) | async-done | bytes 1048592 | tf_op jit(solution)/shard_map/all_gather | solution.py:33
  332.8 1.3 reduce_sum.104
  334.1 0.8 convolution_convert_fusion.8
  335.6 76.4 %all-gather.53.cloned.1.call-done = bf16[4096,256]{1,0:T(8,128)(2,1)} async-done(((bf16[128,256]{1,0:T(8,128)(2,1)}), bf16[4096,256]{1,0:T(8,128)(2,1)}) %all-gather.53.cloned.1.call-update) | async-done | bytes 2097168 | tf_op jit(solution)/shard_map/all_gather | solution.py:41
  412.1 1.0 bitcast_dynamic-update-slice_fusion.5
  413.6 2.2 convolution_bitcast_fusion.6
  415.9 24.4 %all-gather.55.cloned.1.call-done = f32[1024,256]{1,0:T(8,128)} async-done(((f32[128,256]{1,0:T(8,128)}), f32[1024,256]{1,0:T(8,128)}) %all-gather.55.cloned.1.call-update) | async-done | bytes 1048592 | tf_op jit(solution)/shard_map/all_gather | solution.py:33
  440.3 1.3 reduce_sum.106
  441.6 0.8 convolution_convert_fusion.7
  442.5 1.1 iota_compare_fusion.8
  443.6 76.0 %all-gather.57.cloned.1.call-done = bf16[4096,256]{1,0:T(8,128)(2,1)} async-done(((bf16[128,256]{1,0:T(8,128)(2,1)}), bf16[4096,256]{1,0:T(8,128)(2,1)}) %all-gather.57.cloned.1.call-update) | async-done | bytes 2097168 | tf_op jit(solution)/shard_map/all_gather | solution.py:41
  519.6 1.0 bitcast_dynamic-update-slice_fusion.4
  521.2 2.2 convolution_bitcast_fusion.5
  523.5 24.4 %all-gather.59.cloned.1.call-done = f32[1024,256]{1,0:T(8,128)} async-done(((f32[128,256]{1,0:T(8,128)}), f32[1024,256]{1,0:T(8,128)}) %all-gather.59.cloned.1.call-update) | async-done | bytes 1048592 | tf_op jit(solution)/shard_map/all_gather | solution.py:33
  547.9 1.3 reduce_sum.108
  549.2 1.8 convolution_convert_fusion.5
  552.4 75.4 %all-gather.61.cloned.1.call-done = bf16[4096,256]{1,0:T(8,128)(2,1)} async-done(((bf16[128,256]{1,0:T(8,128)(2,1)}), bf16[4096,256]{1,0:T(8,128)(2,1)}) %all-gather.61.cloned.1.call-update) | async-done | bytes 2097168 | tf_op jit(solution)/shard_map/all_gather | solution.py:41
  627.8 1.0 dynamic-slice_bitcast_fusion
  629.5 2.2 convolution_bitcast_fusion.4
  631.8 24.4 %all-gather.63.cloned.1.call-done = f32[1024,256]{1,0:T(8,128)} async-done(((f32[128,256]{1,0:T(8,128)}), f32[1024,256]{1,0:T(8,128)}) %all-gather.63.cloned.1.call-update) | async-done | bytes 1048592 | tf_op jit(solution)/shard_map/all_gather | solution.py:33
  656.2 1.3 reduce_sum.110
  657.5 0.8 convolution_convert_fusion.4
  659.1 76.3 %all-gather.65.cloned.1.call-done = bf16[4096,256]{1,0:T(8,128)(2,1)} async-done(((bf16[128,256]{1,0:T(8,128)(2,1)}), bf16[4096,256]{1,0:T(8,128)(2,1)}) %all-gather.65.cloned.1.call-update) | async-done | bytes 2097168 | tf_op jit(solution)/shard_map/all_gather | solution.py:41
  735.5 1.0 bitcast_dynamic-update-slice_fusion.3
  737.1 2.2 convolution_bitcast_fusion.3
  739.3 24.4 %all-gather.67.cloned.1.call-done = f32[1024,256]{1,0:T(8,128)} async-done(((f32[128,256]{1,0:T(8,128)}), f32[1024,256]{1,0:T(8,128)}) %all-gather.67.cloned.1.call-update) | async-done | bytes 1048592 | tf_op jit(solution)/shard_map/all_gather | solution.py:33
  763.7 1.3 reduce_sum.111
  765.0 0.8 convolution_convert_fusion.3
  766.6 76.2 %all-gather.69.cloned.1.call-done = bf16[4096,256]{1,0:T(8,128)(2,1)} async-done(((bf16[128,256]{1,0:T(8,128)(2,1)}), bf16[4096,256]{1,0:T(8,128)(2,1)}) %all-gather.69.cloned.1.call-update) | async-done | bytes 2097168 | tf_op jit(solution)/shard_map/all_gather | solution.py:41
  842.9 1.0 bitcast_dynamic-update-slice_fusion.2
  844.4 2.2 convolution_bitcast_fusion.2
  846.7 24.4 %all-gather.71.cloned.1.call-done = f32[1024,256]{1,0:T(8,128)} async-done(((f32[128,256]{1,0:T(8,128)}), f32[1024,256]{1,0:T(8,128)}) %all-gather.71.cloned.1.call-update) | async-done | bytes 1048592 | tf_op jit(solution)/shard_map/all_gather | solution.py:33
  871.1 1.3 reduce_sum.112
  872.4 0.8 convolution_convert_fusion.2
  873.9 76.3 %all-gather.73.cloned.1.call-done = bf16[4096,256]{1,0:T(8,128)(2,1)} async-done(((bf16[128,256]{1,0:T(8,128)(2,1)}), bf16[4096,256]{1,0:T(8,128)(2,1)}) %all-gather.73.cloned.1.call-update) | async-done | bytes 2097168 | tf_op jit(solution)/shard_map/all_gather | solution.py:41
  950.2 1.0 bitcast_dynamic-update-slice_fusion.1
  951.8 2.2 convolution_bitcast_fusion.1
  954.1 24.4 %all-gather.75.cloned.1.call-done = f32[1024,256]{1,0:T(8,128)} async-done(((f32[128,256]{1,0:T(8,128)}), f32[1024,256]{1,0:T(8,128)}) %all-gather.75.cloned.1.call-update) | async-done | bytes 1048592 | tf_op jit(solution)/shard_map/all_gather | solution.py:33
  978.4 1.3 reduce_sum.113
  979.8 0.8 convolution_convert_fusion.1
  981.3 76.4 %all-gather.77.cloned.1.call-done = bf16[4096,256]{1,0:T(8,128)(2,1)} async-done(((bf16[128,256]{1,0:T(8,128)(2,1)}), bf16[4096,256]{1,0:T(8,128)(2,1)}) %all-gather.77.cloned.1.call-update) | async-done | bytes 2097168 | tf_op jit(solution)/shard_map/all_gather | solution.py:41
  1057.7 1.0 bitcast_dynamic-update-slice_fusion
  1059.4 2.2 convolution_bitcast_fusion
  1061.6 24.4 %all-gather.79.cloned.1.call-done = f32[1024,256]{1,0:T(8,128)} async-done(((f32[128,256]{1,0:T(8,128)}), f32[1024,256]{1,0:T(8,128)}) %all-gather.79.cloned.1.call-update) | async-done | bytes 1048592 | tf_op jit(solution)/shard_map/all_gather | solution.py:33
  1086.0 1.3 reduce_sum.114
  1087.7 0.7 copy-done.14
  (113 shorter events, 14.0 us)
Async XLA Ops:
  6.5 83.1 %all-gather.41.cloned.1.call-start = ((), (), s32[]{:S(2)}) async-start(), calls=%async_computation | async-start | bytes 2162688 | tf_op jit(solution)/shard_map/all_gather | solution.py:41
  8.3 109.7 %all-gather.43.cloned.1.call-start = ((), (), s32[]{:S(2)}) async-start(), calls=%async_computation.1 | async-start | bytes 1179648 | tf_op jit(solution)/shard_map/all_gather | solution.py:33
  90.7 28.6 %copy-start.1 = (bf16[1,6,256,256]{3,2,1,0:T(8,128)(2,1)S(1)}, bf16[1,6,256,256]{3,2,1,0:T(8,128)(2,1)}, u32[]{:S(2)}) copy-start(bf16[1,6,256,256]{3,2,1,0:T(8,128)(2,1)} %param.30) | copy-start | bytes 2359300
  90.8 28.5 %copy-start.12 = (bf16[1,6,128,256]{3,2,1,0:T(8,128)(2,1)S(1)}, bf16[1,6,128,256]{3,2,1,0:T(8,128)(2,1)}, u32[]{:S(2)}) copy-start(bf16[1,6,128,256]{3,2,1,0:T(8,128)(2,1)} %param.29) | copy-start | bytes 1179652
  93.6 103.7 %all-gather.45.cloned.1.call-start = ((), (), s32[]{:S(2)}) async-start(), calls=%async_computation.2 | async-start | bytes 2162688 | tf_op jit(solution)/shard_map/all_gather | solution.py:41
  120.2 105.3 %all-gather.47.cloned.1.call-start = ((), (), s32[]{:S(2)}) async-start(), calls=%async_computation.3 | async-start | bytes 1179648 | tf_op jit(solution)/shard_map/all_gather | solution.py:33
  201.1 103.6 %all-gather.49.cloned.1.call-start = ((), (), s32[]{:S(2)}) async-start(), calls=%async_computation.4 | async-start | bytes 2162688 | tf_op jit(solution)/shard_map/all_gather | solution.py:41
  227.6 105.2 %all-gather.51.cloned.1.call-start = ((), (), s32[]{:S(2)}) async-start(), calls=%async_computation.5 | async-start | bytes 1179648 | tf_op jit(solution)/shard_map/all_gather | solution.py:33
  308.4 103.7 %all-gather.53.cloned.1.call-start = ((), (), s32[]{:S(2)}) async-start(), calls=%async_computation.6 | async-start | bytes 2162688 | tf_op jit(solution)/shard_map/all_gather | solution.py:41
  335.0 105.3 %all-gather.55.cloned.1.call-start = ((), (), s32[]{:S(2)}) async-start(), calls=%async_computation.7 | async-start | bytes 1179648 | tf_op jit(solution)/shard_map/all_gather | solution.py:33
  415.9 103.7 %all-gather.57.cloned.1.call-start = ((), (), s32[]{:S(2)}) async-start(), calls=%async_computation.8 | async-start | bytes 2162688 | tf_op jit(solution)/shard_map/all_gather | solution.py:41
  442.4 105.4 %all-gather.59.cloned.1.call-start = ((), (), s32[]{:S(2)}) async-start(), calls=%async_computation.9 | async-start | bytes 1179648 | tf_op jit(solution)/shard_map/all_gather | solution.py:33
  519.6 29.6 %copy-start = (bf16[1,6,256,256]{3,2,1,0:T(8,128)(2,1)S(1)}, bf16[1,6,256,256]{3,2,1,0:T(8,128)(2,1)}, u32[]{:S(2)}) copy-start(bf16[1,6,256,256]{3,2,1,0:T(8,128)(2,1)} %param.31) | copy-start | bytes 2359300
  520.6 30.4 %copy-start.13 = (s32[1,5,1]{1,2,0:T(1,128)S(1)}, s32[1,5,1]{1,2,0:T(1,128)}, u32[]{:S(2)}) copy-start(s32[1,5,1]{1,2,0:T(1,128)} %param.37) | copy-start | bytes 64
  521.2 31.2 %copy-start.17 = (s32[6]{0:T(128)S(1)}, s32[6]{0:T(128)}, u32[]{:S(2)}) copy-start(s32[6]{0:T(128)} %get-tuple-element.146) | copy-start | bytes 76
  523.4 104.4 %all-gather.61.cloned.1.call-start = ((), (), s32[]{:S(2)}) async-start(), calls=%async_computation.10 | async-start | bytes 2162688 | tf_op jit(solution)/shard_map/all_gather | solution.py:41
  551.0 105.2 %all-gather.63.cloned.1.call-start = ((), (), s32[]{:S(2)}) async-start(), calls=%async_computation.11 | async-start | bytes 1179648 | tf_op jit(solution)/shard_map/all_gather | solution.py:33
  628.9 28.6 %copy-start.10 = (bf16[128,256]{1,0:T(8,128)(2,1)S(1)}, bf16[128,256]{1,0:T(8,128)(2,1)}, u32[]{:S(2)}) copy-start(bf16[128,256]{1,0:T(8,128)(2,1)} %convolution_convert_fusion.7) | copy-start | bytes 196612
  629.0 30.1 %copy-start.16 = (s32[6]{0:T(128)S(1)}, s32[6]{0:T(128)}, u32[]{:S(2)}) copy-start(s32[6]{0:T(128)} %get-tuple-element.147) | copy-start | bytes 76
  631.8 103.7 %all-gather.65.cloned.1.call-start = ((), (), s32[]{:S(2)}) async-start(), calls=%async_computation.12 | async-start | bytes 2162688 | tf_op jit(solution)/shard_map/all_gather | solution.py:41
  658.4 105.4 %all-gather.67.cloned.1.call-start = ((), (), s32[]{:S(2)}) async-start(), calls=%async_computation.13 | async-start | bytes 1179648 | tf_op jit(solution)/shard_map/all_gather | solution.py:33
  735.5 29.5 %copy-start.9 = (bf16[128,256]{1,0:T(8,128)(2,1)S(1)}, bf16[128,256]{1,0:T(8,128)(2,1)}, u32[]{:S(2)}) copy-start(bf16[128,256]{1,0:T(8,128)(2,1)} %convolution_convert_fusion.8) | copy-start | bytes 196612
  736.5 30.1 %copy-start.15 = (s32[6]{0:T(128)S(1)}, s32[6]{0:T(128)}, u32[]{:S(2)}) copy-start(s32[6]{0:T(128)} %get-tuple-element.148) | copy-start | bytes 76
  739.3 103.6 %all-gather.69.cloned.1.call-start = ((), (), s32[]{:S(2)}) async-start(), calls=%async_computation.14 | async-start | bytes 2162688 | tf_op jit(solution)/shard_map/all_gather | solution.py:41
  765.9 105.2 %all-gather.71.cloned.1.call-start = ((), (), s32[]{:S(2)}) async-start(), calls=%async_computation.15 | async-start | bytes 1179648 | tf_op jit(solution)/shard_map/all_gather | solution.py:33
  842.8 29.5 %copy-start.8 = (bf16[128,256]{1,0:T(8,128)(2,1)S(1)}, bf16[128,256]{1,0:T(8,128)(2,1)}, u32[]{:S(2)}) copy-start(bf16[128,256]{1,0:T(8,128)(2,1)} %convolution_convert_fusion.9) | copy-start | bytes 196612
  846.7 103.6 %all-gather.73.cloned.1.call-start = ((), (), s32[]{:S(2)}) async-start(), calls=%async_computation.16 | async-start | bytes 2162688 | tf_op jit(solution)/shard_map/all_gather | solution.py:41
  873.2 105.2 %all-gather.75.cloned.1.call-start = ((), (), s32[]{:S(2)}) async-start(), calls=%async_computation.17 | async-start | bytes 1179648 | tf_op jit(solution)/shard_map/all_gather | solution.py:33
  950.2 29.5 %copy-start.7 = (bf16[128,256]{1,0:T(8,128)(2,1)S(1)}, bf16[128,256]{1,0:T(8,128)(2,1)}, u32[]{:S(2)}) copy-start(bf16[128,256]{1,0:T(8,128)(2,1)} %convolution_convert_fusion.10) | copy-start | bytes 196612
  954.0 103.7 %all-gather.77.cloned.1.call-start = ((), (), s32[]{:S(2)}) async-start(), calls=%async_computation.18 | async-start | bytes 2162688 | tf_op jit(solution)/shard_map/all_gather | solution.py:41
  980.6 105.4 %all-gather.79.cloned.1.call-start = ((), (), s32[]{:S(2)}) async-start(), calls=%async_computation.19 | async-start | bytes 1179648 | tf_op jit(solution)/shard_map/all_gather | solution.py:33
  1057.7 29.6 %copy-start.6 = (bf16[128,256]{1,0:T(8,128)(2,1)S(1)}, bf16[128,256]{1,0:T(8,128)(2,1)}, u32[]{:S(2)}) copy-start(bf16[128,256]{1,0:T(8,128)(2,1)} %convolution_convert_fusion.11) | copy-start | bytes 196612
  1058.7 28.8 %copy-start.5 = (bf16[128,256]{1,0:T(8,128)(2,1)S(1)}, bf16[128,256]{1,0:T(8,128)(2,1)}, u32[]{:S(2)}) copy-start(bf16[128,256]{1,0:T(8,128)(2,1)} %convolution_convert_fusion.1) | copy-start | bytes 196612
  1058.7 28.8 %copy-start.4 = (bf16[128,256]{1,0:T(8,128)(2,1)S(1)}, bf16[128,256]{1,0:T(8,128)(2,1)}, u32[]{:S(2)}) copy-start(bf16[128,256]{1,0:T(8,128)(2,1)} %convolution_convert_fusion.2) | copy-start | bytes 196612
  1058.7 28.9 %copy-start.3 = (bf16[128,256]{1,0:T(8,128)(2,1)S(1)}, bf16[128,256]{1,0:T(8,128)(2,1)}, u32[]{:S(2)}) copy-start(bf16[128,256]{1,0:T(8,128)(2,1)} %convolution_convert_fusion.3) | copy-start | bytes 196612
  1059.3 28.3 %copy-start.2 = (bf16[128,256]{1,0:T(8,128)(2,1)S(1)}, bf16[128,256]{1,0:T(8,128)(2,1)}, u32[]{:S(2)}) copy-start(bf16[128,256]{1,0:T(8,128)(2,1)} %convolution_convert_fusion.4) | copy-start | bytes 196612
  1059.3 28.3 %copy-start.11 = (bf16[128,256]{1,0:T(8,128)(2,1)S(1)}, bf16[128,256]{1,0:T(8,128)(2,1)}, u32[]{:S(2)}) copy-start(bf16[128,256]{1,0:T(8,128)(2,1)} %convolution_convert_fusion.5) | copy-start | bytes 196612
  1087.7 0.7 copy-start.14
Sparse Core Ops, SparseCore 0:
  9.9 79.6 all-gather.40
  93.7 24.2 all-gather.42
  120.6 76.6 all-gather.44
  201.2 24.2 all-gather.46
  227.9 76.6 all-gather.48
  308.5 24.2 all-gather.50
  335.4 76.6 all-gather.52
  416.0 24.2 all-gather.54
  442.9 76.6 all-gather.56
  523.6 24.2 all-gather.58
  551.1 76.6 all-gather.60
  631.9 24.2 all-gather.62
  658.8 76.6 all-gather.64
  739.4 24.2 all-gather.66
  766.2 76.6 all-gather.68
  846.8 24.2 all-gather.70
  873.5 76.6 all-gather.72
  954.1 24.2 all-gather.74
  981.0 76.6 all-gather.76
  1061.7 24.2 all-gather.78
